TPU v7x, 32 devices: a whole 2x2x4 slice. The times are simulated.
32 devices in a mesh: gx: 16 (over z, y, core), gy: 2 (over x).
Axes of the slice: x: 2, y: 2, z: 4, core: 2. Of those that a mesh axis runs over, the one named last changes fastest.
Arguments:
- field: float32 [6, 16, 256, 256], P(None, None, 'gx', 'gy'), may hold values from -6 to 6
- driver: float32 [6, 16, 256, 256], P(None, None, 'gx', 'gy'), may hold values from -6 to 6
- east_wind: float32 [16, 256, 256], P(None, 'gx', 'gy'), may hold values from -0.4 to 0.4
- north_wind: float32 [16, 256, 256], P(None, 'gx', 'gy'), may hold values from -0.4 to 0.4
Outputs:
- advected: float32 [6, 16, 256, 256], P(None, None, 'gx', 'gy')
- coeffs: float32 [6, 16, 4096], replicated
All inputs are finite; a program needn't handle non-finite values.
Results may differ from a plain program's by a relative error of at most 0.000098.
Values sent between devices are 32-bit elements; how exact they have to be, the bound alone decides.
A program may use at most 128 MiB of HBM per device.

v0:
```python
import math
import jax
import jax.numpy as jnp
from jax import lax
from jax.sharding import PartitionSpec as P

MX = 64
MY = 64


def shifted(value, axis, steps):
    count = lax.axis_size(axis)
    first, last = (max(0, -steps), min(count, count - steps))
    return lax.ppermute(value, axis, [(source, source + steps) for source in range(first, last)])


def padded(x, sides, width):
    for axis, dim in sides:
        peers, length = (lax.axis_size(axis), x.shape[dim])
        up = [(i, (i + 1) % peers) for i in range(peers - 1)]
        down = [(j, i) for i, j in up]
        last = lax.slice_in_dim(x, length - width, length, axis=dim)
        first = lax.slice_in_dim(x, 0, width, axis=dim)
        before = lax.ppermute(last, axis, up)
        after = lax.ppermute(first, axis, down)
        x = jnp.concatenate([before, x, after], axis=dim)
    return x


def cosine_table(first, count, total, modes):
    indices = first + jnp.arange(count, dtype=jnp.int32)
    wavenum = jnp.arange(modes, dtype=jnp.int32)
    phases = (wavenum[None, :] * (2 * indices[:, None] + 1)).astype(jnp.float32)
    cosines = jnp.cos(phases * (math.pi / (2.0 * total)))
    weight = jnp.where(wavenum == 0, math.sqrt(1.0 / total), math.sqrt(2.0 / total)).astype(
        jnp.float32
    )
    return cosines * weight[None, :]


def upwind(tracer, winds):
    east = winds[0]
    north = winds[1]
    east_flux = (
        jnp.maximum(east[:, :-1, :], 0.0) * tracer[..., :-1, :]
        + jnp.minimum(east[:, :-1, :], 0.0) * tracer[..., 1:, :]
    )
    north_flux = (
        jnp.maximum(north[:, :, :-1], 0.0) * tracer[..., :, :-1]
        + jnp.minimum(north[:, :, :-1], 0.0) * tracer[..., :, 1:]
    )
    inner = tracer[..., 1:-1, 1:-1]
    inner = inner - (east_flux[..., 1:, 1:-1] - east_flux[..., :-1, 1:-1])
    return inner - (north_flux[..., 1:-1, 1:] - north_flux[..., 1:-1, :-1])


def shards(field, driver, east_wind, north_wind):
    high = lax.Precision.HIGHEST
    tracers, levels, strip_cols, band_rows = field.shape
    nx_total = strip_cols * lax.axis_size("gx")
    ny_total = band_rows * lax.axis_size("gy")
    x_first = lax.axis_index("gx") * strip_cols
    y_first = lax.axis_index("gy") * band_rows
    x_table = cosine_table(x_first, strip_cols, nx_total, MX)
    y_table = cosine_table(y_first, band_rows, ny_total, MY)
    departure = driver - field
    half_proj = jnp.einsum("tlxy,xm->tlmy", departure, x_table, precision=high)
    partial_modes = jnp.einsum("tlmy,yn->tlmn", half_proj, y_table, precision=high)
    partial_modes = partial_modes.reshape(tracers, levels, MX * MY)
    coeffs = lax.psum(partial_modes, ("gx", "gy"))
    modal = coeffs.reshape(tracers, levels, MX, MY)
    large_scale = jnp.einsum("tlmn,yn->tlmy", modal, y_table, precision=high)
    large_scale = jnp.einsum("tlmy,xm->tlxy", large_scale, x_table, precision=high)
    nudged = field + 0.5 * large_scale
    xpos = x_first + jnp.arange(strip_cols, dtype=jnp.int32)
    ypos = y_first + jnp.arange(band_rows, dtype=jnp.int32)
    east_face = jnp.where(xpos[None, :, None] == nx_total - 1, jnp.float32(0.0), east_wind)
    north_face = jnp.where(ypos[None, None, :] == ny_total - 1, jnp.float32(0.0), north_wind)
    east_below = shifted(east_face[:, -1:, :], "gx", 1)
    north_below = shifted(north_face[:, :, -1:], "gy", 1)
    east_ext = jnp.concatenate([east_below, east_face, jnp.zeros_like(east_below)], axis=1)
    east_ext = jnp.pad(east_ext, ((0, 0), (0, 0), (1, 1)))
    north_ext = jnp.concatenate([north_below, north_face, jnp.zeros_like(north_below)], axis=2)
    north_ext = jnp.pad(north_ext, ((0, 0), (1, 1), (0, 0)))
    wind_ext = jnp.stack([east_ext, north_ext])
    advected = nudged
    for sweep in range(2):
        field_ext = padded(advected, (("gx", 2), ("gy", 3)), 1)
        advected = upwind(field_ext, wind_ext)
    return (advected, coeffs)


def solution(mesh):
    placed = (
        P(None, None, "gx", "gy"),
        P(None, None, "gx", "gy"),
        P(None, "gx", "gy"),
        P(None, "gx", "gy"),
    )
    return jax.shard_map(
        shards,
        mesh=mesh,
        in_specs=placed,
        out_specs=(P(None, None, "gx", "gy"), P()),
        check_vma=False,
    )
```

profile of v0, /device:TPU:8, one launch (start us, length us, event | category | flops | bytes accessed | tf_op | source)
XLA Modules:
  0.0 223.3 jit_solution(13646085363777777054)
XLA Ops:
  7.3 0.5 copy-done.19
  7.8 4.2 %fusion.12 = f32[64,6,16,128]{3,0,2,1:T(8,128)S(1)} fusion(f32[6,16,16,128]{3,2,1,0:T(8,128)} %param.5, f32[6,16,16,128]{3,2,1,0:T(8,128)} %param.4, f32[64]{0:T(128)S(1)} %compare_select_fusion, s32[16]{0:T(128)S(1)} %multiply_add_fusion.1), kind=kOutput, calls=%fused_computation.29 | convolution fusion | flops 151195648 | bytes 4718912 | tf_op jit(solution)/shard_map/tlxy,xm->tlmy/dot_general | solution.py:67
  12.0 2.7 %fusion = f32[6,16,64,64]{3,2,1,0:T(8,128)S(1)} fusion(f32[64,6,16,128]{3,0,2,1:T(8,128)S(1)} %fusion.12, f32[64]{0:T(128)S(1)} %compare_select_fusion, s32[128]{0:T(128)S(1)} %multiply_add_fusion), kind=kOutput, calls=%fused_computation | convolution fusion | flops 604012544 | bytes 4719360 | tf_op jit(solution)/shard_map/tlmy,yn->tlmn/dot_general | solution.py:68
  14.7 1.9 reshape.47
  16.8 3.4 %collective-permute-start.5 = (f32[16,16,1]{2,1,0:T(8,128)S(1)}, f32[16,16,1]{2,1,0:T(8,128)S(1)}, u32[]{:S(2)}, u32[]{:S(2)}) collective-permute-start(f32[16,16,1]{2,1,0:T(8,128)S(1)} %slice.119), channel_id=1, source_target_pairs={{0,1},{2,3},{4,5},{6,7},{8,9},{10,11},{12,13},{14,15},{16,17},{18,... | collective-permute-start | bytes 3080 | tf_op jit(solution)/shard_map/ppermute | solution.py:14
  20.3 2.1 collective-permute-start
  22.5 0.7 pad.47.clone
  23.3 0.8 fusion.17
  24.1 125.8 %all-reduce.4.cloned.1.call-done = f32[6,16,4096]{2,1,0:T(8,128)} async-done(((f32[6,16,4096]{2,1,0:T(8,128)}), f32[6,16,4096]{2,1,0:T(8,128)}) %all-reduce.4.cloned.1.call-update) | async-done | bytes 1572880 | tf_op jit(solution)/shard_map/psum | solution.py:70
  149.9 2.4 %reshape.48 = f32[6,16,64,64]{3,2,1,0:T(8,128)S(1)} reshape(f32[6,16,4096]{2,1,0:T(8,128)} %all-reduce.4.cloned.1.call-done) | data formatting | bytes 3145728 | tf_op jit(solution)/shard_map/reshape | solution.py:71
  152.3 3.6 %fusion.18 = f32[6,16,64,128]{3,2,1,0:T(8,128)S(1)} fusion(f32[6,16,64,64]{3,2,1,0:T(8,128)S(1)} %reshape.48, f32[64]{0:T(128)} %copy-done.17, s32[128]{0:T(128)} %copy-done.21), kind=kOutput, calls=%fused_computation.41 | convolution fusion | flops 604012544 | bytes 4719360 | tf_op jit(solution)/shard_map/tlmn,yn->tlmy/dot_general | solution.py:72
  156.0 1.7 fusion.7
  157.7 1.9 collective-permute-start.2
  159.7 2.4 %collective-permute-start.1 = (f32[6,16,1,128]{3,2,1,0:T(1,128)S(1)}, f32[6,16,1,128]{3,2,1,0:T(1,128)S(1)}, u32[]{:S(2)}, u32[]{:S(2)}) collective-permute-start(f32[6,16,1,128]{3,2,1,0:T(1,128)S(1)} %get-tuple-element.8), channel_id=1, source_target_pairs={{0,2},{2,4},{4,6},{6,8},{8,10},{10,12},{12,14},{14,16},{16,18},{18... | collective-permute-start | bytes 147464 | tf_op jit(solution)/shard_map/ppermute | solution.py:24
  162.1 0.8 maximum_maximum_fusion.1
  162.9 3.1 %collective-permute-done.1 = f32[6,16,1,128]{3,2,1,0:T(1,128)S(1)} collective-permute-done((f32[6,16,1,128]{3,2,1,0:T(1,128)S(1)}, f32[6,16,1,128]{3,2,1,0:T(1,128)S(1)}, u32[]{:S(2)}, u32[]{:S(2)}) %collective-permute-start.1) | collective-permute-done | bytes 49184 | tf_op jit(solution)/shard_map/ppermute | solution.py:24
  166.0 0.2 pad_maximum_fusion.2
  166.2 0.4 fusion.42
  166.6 1.3 copy.6
  167.9 3.3 %collective-permute-start.3 = (f32[6,16,18,1]{2,1,3,0:T(8,128)}, f32[6,16,18,1]{2,1,3,0:T(8,128)S(1)}, u32[]{:S(2)}, u32[]{:S(2)}) collective-permute-start(f32[6,16,18,1]{2,1,3,0:T(8,128)} %copy.6), channel_id=1, source_target_pairs={{0,1},{2,3},{4,5},{6,7},{8,9},{10,11},{12,13},{14,15},{16,17},{18,... | collective-permute-start | bytes 20744 | tf_op jit(solution)/shard_map/ppermute | solution.py:24
  171.2 0.7 copy.7
  171.9 1.3 collective-permute-start.4
  173.1 2.2 fusion.15
  175.3 0.7 copy.8
  176.0 1.9 collective-permute-done.4
  177.9 1.5 copy.9
  179.4 2.3 %pad_maximum_fusion = f32[6,16,18,130]{3,2,1,0:T(8,128)S(1)} fusion(f32[6,16,18,1]{3,2,1,0:T(8,128)S(1)} %copy.9, f32[6,16,1,128]{3,2,1,0:T(1,128)} %copy-done.11, f32[6,16,16,128]{3,2,1,0:T(8,128)S(1)} %fusion.7, f32[6,16,1,128]{3,2,1,0:T(1,128)} %copy-done.13, f32[6,16,18,1]{3,2,1,0:T(8,128)S(1)} %copy.8), kind=kLoop, calls=%fused_computation.8 | loop fusion | flops 898560 | bytes 1797120 | tf_op jit(solution)/shard_map/concatenate | solution.py:26
  181.8 0.4 fusion.3
  182.2 0.5 copy-done.2
  182.8 1.3 fusion.4
  184.0 0.7 fusion.10
  184.8 1.9 collective-permute-start.7
  186.7 2.6 %collective-permute-start.6 = (f32[6,16,1,128]{3,2,1,0:T(1,128)S(1)}, f32[6,16,1,128]{3,2,1,0:T(1,128)S(1)}, u32[]{:S(2)}, u32[]{:S(2)}) collective-permute-start(f32[6,16,1,128]{3,2,1,0:T(1,128)S(1)} %get-tuple-element.6), channel_id=1, source_target_pairs={{0,2},{2,4},{4,6},{6,8},{8,10},{10,12},{12,14},{14,16},{16,18},{18... | collective-permute-start | bytes 147464 | tf_op jit(solution)/shard_map/ppermute | solution.py:24
  189.3 3.9 %collective-permute-done.6 = f32[6,16,1,128]{3,2,1,0:T(1,128)S(1)} collective-permute-done((f32[6,16,1,128]{3,2,1,0:T(1,128)S(1)}, f32[6,16,1,128]{3,2,1,0:T(1,128)S(1)}, u32[]{:S(2)}, u32[]{:S(2)}) %collective-permute-start.6) | collective-permute-done | bytes 49184 | tf_op jit(solution)/shard_map/ppermute | solution.py:24
  193.4 1.4 fusion.41
  194.8 1.9 copy.12
  196.7 3.2 %collective-permute-start.8 = (f32[6,16,18,1]{2,1,3,0:T(8,128)S(1)}, f32[6,16,18,1]{2,1,3,0:T(8,128)S(1)}, u32[]{:S(2)}, u32[]{:S(2)}) collective-permute-start(f32[6,16,18,1]{2,1,3,0:T(8,128)S(1)} %copy.12), channel_id=1, source_target_pairs={{0,1},{2,3},{4,5},{6,7},{8,9},{10,11},{12,13},{14,15},{16,17},{18,... | collective-permute-start | bytes 20744 | tf_op jit(solution)/shard_map/ppermute | solution.py:24
  200.0 0.7 copy.13
  200.7 1.3 collective-permute-start.9
  202.0 0.7 copy.14
  202.7 4.0 %collective-permute-done.9 = f32[6,16,18,1]{2,1,3,0:T(8,128)S(1)} collective-permute-done((f32[6,16,18,1]{2,1,3,0:T(8,128)S(1)}, f32[6,16,18,1]{2,1,3,0:T(8,128)S(1)}, u32[]{:S(2)}, u32[]{:S(2)}) %collective-permute-start.9) | collective-permute-done | bytes 6944 | tf_op jit(solution)/shard_map/ppermute | solution.py:25
  206.6 1.7 copy.15
  208.3 2.7 %pad_maximum_fusion.1 = f32[6,16,18,130]{3,2,1,0:T(8,128)S(1)} fusion(f32[6,16,18,1]{3,2,1,0:T(8,128)} %copy.15, f32[6,16,1,128]{3,2,1,0:T(1,128)S(1)} %collective-permute-done.7, f32[6,16,16,128]{3,2,1,0:T(8,128)S(1)} %fusion.10, f32[6,16,1,128]{3,2,1,0:T(1,128)S(1)} %collective-permute-done.6, f32[6,16,18,1]{3,2,1,0:T(8,128)S(1)} %copy.14), kind=kLoop, calls=%fused_computation.12 | loop fusion | flops 898560 | bytes 1797120 | tf_op jit(solution)/shard_map/concatenate | solution.py:26
  211.1 0.4 fusion.2
  211.6 0.8 copy-done
  212.4 1.3 fusion.5
  213.7 1.6 fusion.8
  215.3 1.1 copy.21
  (65 shorter events, 1.0 us)
Async XLA Ops:
  7.2 142.7 %all-reduce.4.cloned.1.call-start = ((), (), s32[]{:S(2)}) async-start(), calls=%async_computation | async-start | bytes 3145728 | tf_op jit(solution)/shard_map/psum | solution.py:70
  7.2 4.7 %copy-start.17 = (f32[64]{0:T(128)}, f32[64]{0:T(128)S(1)}, u32[]{:S(2)}) copy-start(f32[64]{0:T(128)S(1)} %compare_select_fusion) | copy-start | bytes 772
  7.2 0.5 copy-start.19
  7.8 4.2 %copy-start.21 = (s32[128]{0:T(128)}, s32[128]{0:T(128)S(1)}, u32[]{:S(2)}) copy-start(s32[128]{0:T(128)S(1)} %multiply_add_fusion) | copy-start | bytes 1540
  14.7 2.0 copy-start.15
  14.7 5.5 %copy-start.16 = (f32[16,16,128]{2,1,0:T(8,128)S(1)}, f32[16,16,128]{2,1,0:T(8,128)}, u32[]{:S(2)}) copy-start(f32[16,16,128]{2,1,0:T(8,128)} %param.6) | copy-start | bytes 393220
  16.8 6.4 %collective-permute-start.5 = (f32[16,16,1]{2,1,0:T(8,128)S(1)}, f32[16,16,1]{2,1,0:T(8,128)S(1)}, u32[]{:S(2)}, u32[]{:S(2)}) collective-permute-start(f32[16,16,1]{2,1,0:T(8,128)S(1)} %slice.119), channel_id=1, source_target_pairs={{0,1},{2,3},{4,5},{6,7},{8,9},{10,11},{12,13},{14,15},{16,17},{18,... | collective-permute-start | bytes 3080 | tf_op jit(solution)/shard_map/ppermute | solution.py:14
  20.3 2.9 %copy-start.9 = (f32[16,16,128]{2,1,0:T(8,128)}, f32[16,16,128]{2,1,0:T(8,128)S(1)}, u32[]{:S(2)}) copy-start(f32[16,16,128]{2,1,0:T(8,128)S(1)} %broadcast_select_fusion.1) | copy-start | bytes 393220
  20.3 141.7 %collective-permute-start = (f32[16,1,128]{2,1,0:T(1,128)S(1)}, f32[16,1,128]{2,1,0:T(1,128)S(1)}, u32[]{:S(2)}, u32[]{:S(2)}) collective-permute-start(f32[16,1,128]{2,1,0:T(1,128)S(1)} %slice.110), channel_id=1, source_target_pairs={{0,2},{2,4},{4,6},{6,8},{8,10},{10,12},{12,14},{14,16},{16,18},{18... | collective-permute-start | bytes 24584 | tf_op jit(solution)/shard_map/ppermute | solution.py:14
  152.3 3.6 %copy-start.8 = (f32[6,16,16,128]{3,2,1,0:T(8,128)S(1)}, f32[6,16,16,128]{3,2,1,0:T(8,128)}, u32[]{:S(2)}) copy-start(f32[6,16,16,128]{3,2,1,0:T(8,128)} %param.4) | copy-start | bytes 2359300
  152.3 3.6 %copy-start.18 = (f32[64]{0:T(128)S(1)}, f32[64]{0:T(128)}, u32[]{:S(2)}) copy-start(f32[64]{0:T(128)} %copy-done.17) | copy-start | bytes 772
  152.3 3.6 %copy-start.20 = (s32[16]{0:T(128)S(1)}, s32[16]{0:T(128)}, u32[]{:S(2)}) copy-start(s32[16]{0:T(128)} %copy-done.19) | copy-start | bytes 196
  155.9 6.1 %copy-start.10 = (f32[16,16,128]{2,1,0:T(8,128)S(1)}, f32[16,16,128]{2,1,0:T(8,128)}, u32[]{:S(2)}) copy-start(f32[16,16,128]{2,1,0:T(8,128)} %copy-done.9) | copy-start | bytes 393220
  156.0 6.1 %copy-start.22 = (f32[18]{0:T(128)S(1)}, f32[18]{0:T(128)}, u32[]{:S(2)}) copy-start(f32[18]{0:T(128)} %pad.47.clone) | copy-start | bytes 220
  157.7 5.1 %collective-permute-start.2 = (f32[6,16,1,128]{3,2,1,0:T(1,128)S(1)}, f32[6,16,1,128]{3,2,1,0:T(1,128)S(1)}, u32[]{:S(2)}, u32[]{:S(2)}) collective-permute-start(f32[6,16,1,128]{3,2,1,0:T(1,128)S(1)} %get-tuple-element.9), channel_id=1, source_target_pairs={{2,0},{4,2},{6,4},{8,6},{10,8},{12,10},{14,12},{16,14},{18,16},{20... | collective-permute-start | bytes 147464 | tf_op jit(solution)/shard_map/ppermute | solution.py:25
  159.7 6.3 %collective-permute-start.1 = (f32[6,16,1,128]{3,2,1,0:T(1,128)S(1)}, f32[6,16,1,128]{3,2,1,0:T(1,128)S(1)}, u32[]{:S(2)}, u32[]{:S(2)}) collective-permute-start(f32[6,16,1,128]{3,2,1,0:T(1,128)S(1)} %get-tuple-element.8), channel_id=1, source_target_pairs={{0,2},{2,4},{4,6},{6,8},{8,10},{10,12},{12,14},{14,16},{16,18},{18... | collective-permute-start | bytes 147464 | tf_op jit(solution)/shard_map/ppermute | solution.py:24
  162.9 3.7 %copy-start.11 = (f32[6,16,1,128]{3,2,1,0:T(1,128)}, f32[6,16,1,128]{3,2,1,0:T(1,128)S(1)}, u32[]{:S(2)}) copy-start(f32[6,16,1,128]{3,2,1,0:T(1,128)S(1)} %collective-permute-done.2) | copy-start | bytes 147460
  166.0 0.6 copy-start.13
  167.9 7.5 %collective-permute-start.3 = (f32[6,16,18,1]{2,1,3,0:T(8,128)}, f32[6,16,18,1]{2,1,3,0:T(8,128)S(1)}, u32[]{:S(2)}, u32[]{:S(2)}) collective-permute-start(f32[6,16,18,1]{2,1,3,0:T(8,128)} %copy.6), channel_id=1, source_target_pairs={{0,1},{2,3},{4,5},{6,7},{8,9},{10,11},{12,13},{14,15},{16,17},{18,... | collective-permute-start | bytes 20744 | tf_op jit(solution)/shard_map/ppermute | solution.py:24
  171.9 6.1 %collective-permute-start.4 = (f32[6,16,18,1]{2,1,3,0:T(8,128)S(1)}, f32[6,16,18,1]{2,1,3,0:T(8,128)}, u32[]{:S(2)}, u32[]{:S(2)}) collective-permute-start(f32[6,16,18,1]{2,1,3,0:T(8,128)S(1)} %copy.7), channel_id=1, source_target_pairs={{1,0},{3,2},{5,4},{7,6},{9,8},{11,10},{13,12},{15,14},{17,16},{19,... | collective-permute-start | bytes 20744 | tf_op jit(solution)/shard_map/ppermute | solution.py:25
  179.4 2.3 %copy-start.4 = (f32[16,17,130]{2,1,0:T(8,128)S(1)}, f32[16,17,130]{2,1,0:T(8,128)}, u32[]{:S(2)}) copy-start(f32[16,17,130]{2,1,0:T(8,128)} %get-tuple-element.12) | copy-start | bytes 424324
  179.4 2.3 %copy-start.6 = (f32[16,17,130]{2,1,0:T(8,128)S(1)}, f32[16,17,130]{2,1,0:T(8,128)}, u32[]{:S(2)}) copy-start(f32[16,17,130]{2,1,0:T(8,128)} %get-tuple-element.13) | copy-start | bytes 424324
  181.8 1.0 copy-start.2
  181.8 1.0 copy-start.12
  181.8 1.0 copy-start.14
  184.8 4.6 %collective-permute-start.7 = (f32[6,16,1,128]{3,2,1,0:T(1,128)S(1)}, f32[6,16,1,128]{3,2,1,0:T(1,128)S(1)}, u32[]{:S(2)}, u32[]{:S(2)}) collective-permute-start(f32[6,16,1,128]{3,2,1,0:T(1,128)S(1)} %get-tuple-element.7), channel_id=1, source_target_pairs={{2,0},{4,2},{6,4},{8,6},{10,8},{12,10},{14,12},{16,14},{18,16},{20... | collective-permute-start | bytes 147464 | tf_op jit(solution)/shard_map/ppermute | solution.py:25
  186.7 6.5 %collective-permute-start.6 = (f32[6,16,1,128]{3,2,1,0:T(1,128)S(1)}, f32[6,16,1,128]{3,2,1,0:T(1,128)S(1)}, u32[]{:S(2)}, u32[]{:S(2)}) collective-permute-start(f32[6,16,1,128]{3,2,1,0:T(1,128)S(1)} %get-tuple-element.6), channel_id=1, source_target_pairs={{0,2},{2,4},{4,6},{6,8},{8,10},{10,12},{12,14},{14,16},{16,18},{18... | collective-permute-start | bytes 147464 | tf_op jit(solution)/shard_map/ppermute | solution.py:24
  196.7 5.2 %collective-permute-start.8 = (f32[6,16,18,1]{2,1,3,0:T(8,128)S(1)}, f32[6,16,18,1]{2,1,3,0:T(8,128)S(1)}, u32[]{:S(2)}, u32[]{:S(2)}) collective-permute-start(f32[6,16,18,1]{2,1,3,0:T(8,128)S(1)} %copy.12), channel_id=1, source_target_pairs={{0,1},{2,3},{4,5},{6,7},{8,9},{10,11},{12,13},{14,15},{16,17},{18,... | collective-permute-start | bytes 20744 | tf_op jit(solution)/shard_map/ppermute | solution.py:24
  200.7 6.0 %collective-permute-start.9 = (f32[6,16,18,1]{2,1,3,0:T(8,128)S(1)}, f32[6,16,18,1]{2,1,3,0:T(8,128)S(1)}, u32[]{:S(2)}, u32[]{:S(2)}) collective-permute-start(f32[6,16,18,1]{2,1,3,0:T(8,128)S(1)} %copy.13), channel_id=1, source_target_pairs={{1,0},{3,2},{5,4},{7,6},{9,8},{11,10},{13,12},{15,14},{17,16},{19,... | collective-permute-start | bytes 20744 | tf_op jit(solution)/shard_map/ppermute | solution.py:25
  208.3 2.7 %copy-start.5 = (f32[16,17,130]{2,1,0:T(8,128)S(1)}, f32[16,17,130]{2,1,0:T(8,128)}, u32[]{:S(2)}) copy-start(f32[16,17,130]{2,1,0:T(8,128)} %get-tuple-element.12) | copy-start | bytes 424324
  208.3 2.8 %copy-start.7 = (f32[16,17,130]{2,1,0:T(8,128)S(1)}, f32[16,17,130]{2,1,0:T(8,128)}, u32[]{:S(2)}) copy-start(f32[16,17,130]{2,1,0:T(8,128)} %get-tuple-element.13) | copy-start | bytes 424324
  211.1 1.3 copy-start
  211.1 1.3 copy-start.3
  213.7 1.6 copy-start.1
Sparse Core Ops, SparseCore 0:
  16.8 133.0 all-reduce.3
where the time goes:
time: 224 us; the launch traced here: 223 us
  waiting for transfers between devices  139 us (62%)
  starting transfers between devices  23.5 us (10%)
  local copies, waits for them, and re-layouts  19.4 us (9%)
  other arithmetic  15 us (7%)
  between operations  14.6 us (7%)
  matrix products  12.1 us (5%)
    psum x1, waiting for transfers between devices, shards(): coeffs = lax.psum(partial_modes, ('gx', 'gy'))  126 us
    ppermute x4, starting transfers between devices, padded(): before = lax.ppermute(last, axis, up)  11.6 us
    ppermute x4, waiting for transfers between devices, padded(): before = lax.ppermute(last, axis, up)  6.99 us
    ppermute x4, starting transfers between devices, padded(): after = lax.ppermute(first, axis, down)  6.4 us
    ppermute x4, waiting for transfers between devices, padded(): after = lax.ppermute(first, axis, down)  5.89 us
    ppermute x2, starting transfers between devices, shifted(): lax.ppermute(value, axis, [(source, source + steps) for source in range(f...  5.5 us
    concatenate x4, other arithmetic, padded(): x = jnp.concatenate([before, x, after], axis=dim)  5.4 us
  transfers between devices with their start and end apart: 11, of which 5 were waited for; matrix products, arithmetic and copies ran while one was open for 7% of the time, Pallas kernels for 0%

commit v1 on v0

--- a/solution.py
+++ b/solution.py
@@ -1,3 +1,4 @@
+import functools
 import math
 import jax
 import jax.numpy as jnp
@@ -6,6 +7,13 @@
 
 MX = 64
 MY = 64
+
+
+def tell_tables(panel, axis_name):
+    return jnp.sum(lax.all_gather(panel, axis_name), axis=0)
+
+
+_link_quotas = functools.partial(tell_tables, axis_name=("gx", "gy"))
 
 
 def shifted(value, axis, steps):
@@ -67,7 +75,7 @@
     half_proj = jnp.einsum("tlxy,xm->tlmy", departure, x_table, precision=high)
     partial_modes = jnp.einsum("tlmy,yn->tlmn", half_proj, y_table, precision=high)
     partial_modes = partial_modes.reshape(tracers, levels, MX * MY)
-    coeffs = lax.psum(partial_modes, ("gx", "gy"))
+    coeffs = _link_quotas(partial_modes)
     modal = coeffs.reshape(tracers, levels, MX, MY)
     large_scale = jnp.einsum("tlmn,yn->tlmy", modal, y_table, precision=high)
     large_scale = jnp.einsum("tlmy,xm->tlxy", large_scale, x_table, precision=high)

time: 224 us -> 384 us (1.71)
  waiting for transfers between devices: 139 us -> 276 us
  other arithmetic: 15 us -> 33.1 us
  starting transfers between devices: 23.5 us -> 27.8 us
    all_gather x0 -> x1, waiting for transfers between devices: none -> 268 us  [tell_tables(): return jnp.sum(lax.all_gather(panel, axis_name), axis=0)]
    psum x1 -> x0, waiting for transfers between devices: 126 us -> none  [shards(): coeffs = lax.psum(partial_modes, ('gx', 'gy'))]
    reduce_sum x0 -> x1, other arithmetic: none -> 18.1 us  [tell_tables(): return jnp.sum(lax.all_gather(panel, axis_name), axis=0)]
    ppermute x4, waiting for transfers between devices: 6.99 us -> 0.16 us  [padded(): before = lax.ppermute(last, axis, up)]
    ppermute x4, starting transfers between devices: 6.4 us -> 12.2 us  [padded(): after = lax.ppermute(first, axis, down)]
  transfers between devices with their start and end apart: 11 -> 11, of which waited for: 5 -> 6; matrix products, arithmetic and copies ran while one was open for 7% -> 9% of each run, Pallas kernels for 0% -> 0%
where the time goes in v1:
time: 384 us; the launch traced here: 383 us
  waiting for transfers between devices  276 us (72%)
  other arithmetic  33.1 us (9%)
  starting transfers between devices  27.8 us (7%)
  local copies, waits for them, and re-layouts  18.9 us (5%)
  between operations  14.5 us (4%)
  matrix products  12.2 us (3%)
    all_gather x1, waiting for transfers between devices, tell_tables(): return jnp.sum(lax.all_gather(panel, axis_name), axis=0)  268 us
    reduce_sum x1, other arithmetic, tell_tables(): return jnp.sum(lax.all_gather(panel, axis_name), axis=0)  18.1 us
    ppermute x4, starting transfers between devices, padded(): after = lax.ppermute(first, axis, down)  12.2 us
    ppermute x4, starting transfers between devices, padded(): before = lax.ppermute(last, axis, up)  10.1 us
    ppermute x4, waiting for transfers between devices, padded(): after = lax.ppermute(first, axis, down)  8.42 us
  transfers between devices with their start and end apart: 11, of which 6 were waited for; matrix products, arithmetic and copies ran while one was open for 9% of the time, Pallas kernels for 0%

profile of v1, /device:TPU:8, one launch (start us, length us, event | category | flops | bytes accessed | tf_op | source)
XLA Modules:
  0.0 382.7 jit_solution(10335583160947738923)
XLA Ops:
  7.3 0.5 copy-done.18
  7.8 4.2 %fusion.12 = f32[64,6,16,128]{3,0,2,1:T(8,128)S(1)} fusion(f32[6,16,16,128]{3,2,1,0:T(8,128)} %param.5, f32[6,16,16,128]{3,2,1,0:T(8,128)} %param.4, f32[64]{0:T(128)S(1)} %compare_select_fusion, s32[16]{0:T(128)S(1)} %multiply_add_fusion.1), kind=kOutput, calls=%fused_computation.29 | convolution fusion | flops 151195648 | bytes 4718912 | tf_op jit(solution)/shard_map/tlxy,xm->tlmy/dot_general | solution.py:75
  12.0 2.7 fusion
  14.7 1.9 all_gather_reshape.3
  16.8 3.4 collective-permute-start.5
  20.4 2.1 collective-permute-start
  22.5 0.7 pad.47.clone
  23.4 0.8 fusion.17
  24.2 267.5 %all-gather.2.cloned.1.call-done = f32[32,6,16,4096]{3,2,1,0:T(8,128)} async-done(((f32[1,6,16,4096]{3,2,1,0:T(8,128)}), f32[32,6,16,4096]{3,2,1,0:T(8,128)}) %all-gather.2.cloned.1.call-update) | async-done | bytes 50331664 | tf_op jit(solution)/shard_map/all_gather | solution.py:13
  291.7 18.1 %reduce_sum.9 = f32[6,16,4096]{2,1,0:T(8,128)} reduce(f32[32,6,16,4096]{3,2,1,0:T(8,128)} %all-gather.2.cloned.1.call-done, f32[]{:T(128)} %constant.4.clone.1), dimensions={0}, to_apply=%region_0.1 | reduce | flops 12189696 | bytes 51904516 | tf_op jit(solution)/shard_map/reduce_sum | solution.py:13
  309.8 2.4 reshape.44
  312.2 3.6 fusion.18
  315.9 1.7 fusion.7
  317.7 2.2 collective-permute-start.1
  319.9 4.8 %collective-permute-start.2 = (f32[6,16,1,128]{3,2,1,0:T(1,128)S(1)}, f32[6,16,1,128]{3,2,1,0:T(1,128)S(1)}, u32[]{:S(2)}, u32[]{:S(2)}) collective-permute-start(f32[6,16,1,128]{3,2,1,0:T(1,128)S(1)} %get-tuple-element.9), channel_id=1, source_target_pairs={{2,0},{4,2},{6,4},{8,6},{10,8},{12,10},{14,12},{16,14},{18,16},{20... | collective-permute-start | bytes 147464 | tf_op jit(solution)/shard_map/ppermute | solution.py:33
  324.8 0.8 maximum_maximum_fusion.1
  325.5 0.9 collective-permute-done.2
  326.5 0.6 copy-done.12
  327.3 0.4 fusion.42
  327.6 1.3 copy.6
  328.9 2.8 collective-permute-start.3
  331.7 0.7 copy.7
  332.4 1.5 collective-permute-start.4
  333.9 2.2 fusion.15
  336.1 0.7 copy.8
  336.8 1.7 collective-permute-done.4
  338.5 1.5 copy.9
  340.0 2.3 pad_maximum_fusion
  342.3 0.4 fusion.3
  342.7 0.5 copy-done.1
  343.3 1.3 fusion.4
  344.5 0.7 fusion.10
  345.3 1.9 collective-permute-start.6
  347.2 4.5 %collective-permute-start.7 = (f32[6,16,1,128]{3,2,1,0:T(1,128)S(1)}, f32[6,16,1,128]{3,2,1,0:T(1,128)S(1)}, u32[]{:S(2)}, u32[]{:S(2)}) collective-permute-start(f32[6,16,1,128]{3,2,1,0:T(1,128)S(1)} %get-tuple-element.7), channel_id=1, source_target_pairs={{2,0},{4,2},{6,4},{8,6},{10,8},{12,10},{14,12},{16,14},{18,16},{20... | collective-permute-start | bytes 147464 | tf_op jit(solution)/shard_map/ppermute | solution.py:33
  351.8 1.7 collective-permute-done.7
  353.7 1.4 fusion.41
  355.1 1.9 copy.12
  357.0 3.2 collective-permute-start.8
  360.3 0.7 copy.13
  361.0 1.3 collective-permute-start.9
  362.4 0.7 copy.14
  363.1 4.1 %collective-permute-done.9 = f32[6,16,18,1]{2,1,3,0:T(8,128)S(1)} collective-permute-done((f32[6,16,18,1]{2,1,3,0:T(8,128)S(1)}, f32[6,16,18,1]{2,1,3,0:T(8,128)S(1)}, u32[]{:S(2)}, u32[]{:S(2)}) %collective-permute-start.9) | collective-permute-done | bytes 6944 | tf_op jit(solution)/shard_map/ppermute | solution.py:33
  367.2 1.7 copy.15
  368.9 2.7 pad_maximum_fusion.1
  371.7 0.4 fusion.2
  372.2 0.8 copy-done
  373.0 1.3 fusion.5
  374.3 1.6 fusion.8
  (63 shorter events, 1.3 us)
Async XLA Ops:
  7.2 284.5 %all-gather.2.cloned.1.call-start = ((), (), s32[]{:S(2)}) async-start(), calls=%async_computation | async-start | bytes 51904512 | tf_op jit(solution)/shard_map/all_gather | solution.py:13
  7.2 4.7 %copy-start.16 = (f32[64]{0:T(128)}, f32[64]{0:T(128)S(1)}, u32[]{:S(2)}) copy-start(f32[64]{0:T(128)S(1)} %compare_select_fusion) | copy-start | bytes 772
  7.2 0.5 copy-start.18
  7.8 4.2 %copy-start.20 = (s32[128]{0:T(128)}, s32[128]{0:T(128)S(1)}, u32[]{:S(2)}) copy-start(s32[128]{0:T(128)S(1)} %multiply_add_fusion) | copy-start | bytes 1540
  14.7 2.0 copy-start.14
  14.7 5.5 %copy-start.15 = (f32[16,16,128]{2,1,0:T(8,128)S(1)}, f32[16,16,128]{2,1,0:T(8,128)}, u32[]{:S(2)}) copy-start(f32[16,16,128]{2,1,0:T(8,128)} %param.6) | copy-start | bytes 393220
  16.8 6.4 %collective-permute-start.5 = (f32[16,16,1]{2,1,0:T(8,128)S(1)}, f32[16,16,1]{2,1,0:T(8,128)S(1)}, u32[]{:S(2)}, u32[]{:S(2)}) collective-permute-start(f32[16,16,1]{2,1,0:T(8,128)S(1)} %slice.119), channel_id=1, source_target_pairs={{0,1},{2,3},{4,5},{6,7},{8,9},{10,11},{12,13},{14,15},{16,17},{18,... | collective-permute-start | bytes 3080 | tf_op jit(solution)/shard_map/ppermute | solution.py:22
  20.3 2.9 copy-start.8
  20.4 304.4 %collective-permute-start = (f32[16,1,128]{2,1,0:T(1,128)S(1)}, f32[16,1,128]{2,1,0:T(1,128)S(1)}, u32[]{:S(2)}, u32[]{:S(2)}) collective-permute-start(f32[16,1,128]{2,1,0:T(1,128)S(1)} %slice.110), channel_id=1, source_target_pairs={{0,2},{2,4},{4,6},{6,8},{8,10},{10,12},{12,14},{14,16},{16,18},{18... | collective-permute-start | bytes 24584 | tf_op jit(solution)/shard_map/ppermute | solution.py:22
  312.2 3.7 copy-start.7
  312.2 3.7 copy-start.17
  312.2 3.7 copy-start.19
  315.9 8.8 %copy-start.9 = (f32[16,16,128]{2,1,0:T(8,128)S(1)}, f32[16,16,128]{2,1,0:T(8,128)}, u32[]{:S(2)}) copy-start(f32[16,16,128]{2,1,0:T(8,128)} %copy-done.8) | copy-start | bytes 393220
  315.9 8.8 %copy-start.21 = (f32[18]{0:T(128)S(1)}, f32[18]{0:T(128)}, u32[]{:S(2)}) copy-start(f32[18]{0:T(128)} %pad.47.clone) | copy-start | bytes 220
  317.7 7.8 %collective-permute-start.1 = (f32[6,16,1,128]{3,2,1,0:T(1,128)S(1)}, f32[6,16,1,128]{3,2,1,0:T(1,128)S(1)}, u32[]{:S(2)}, u32[]{:S(2)}) collective-permute-start(f32[6,16,1,128]{3,2,1,0:T(1,128)S(1)} %get-tuple-element.8), channel_id=1, source_target_pairs={{0,2},{2,4},{4,6},{6,8},{8,10},{10,12},{12,14},{14,16},{16,18},{18... | collective-permute-start | bytes 147464 | tf_op jit(solution)/shard_map/ppermute | solution.py:32
  319.9 6.6 %collective-permute-start.2 = (f32[6,16,1,128]{3,2,1,0:T(1,128)S(1)}, f32[6,16,1,128]{3,2,1,0:T(1,128)S(1)}, u32[]{:S(2)}, u32[]{:S(2)}) collective-permute-start(f32[6,16,1,128]{3,2,1,0:T(1,128)S(1)} %get-tuple-element.9), channel_id=1, source_target_pairs={{2,0},{4,2},{6,4},{8,6},{10,8},{12,10},{14,12},{16,14},{18,16},{20... | collective-permute-start | bytes 147464 | tf_op jit(solution)/shard_map/ppermute | solution.py:33
  325.5 0.9 copy-start.10
  326.5 0.6 copy-start.12
  328.9 7.1 %collective-permute-start.3 = (f32[6,16,18,1]{2,1,3,0:T(8,128)}, f32[6,16,18,1]{2,1,3,0:T(8,128)S(1)}, u32[]{:S(2)}, u32[]{:S(2)}) collective-permute-start(f32[6,16,18,1]{2,1,3,0:T(8,128)} %copy.6), channel_id=1, source_target_pairs={{0,1},{2,3},{4,5},{6,7},{8,9},{10,11},{12,13},{14,15},{16,17},{18,... | collective-permute-start | bytes 20744 | tf_op jit(solution)/shard_map/ppermute | solution.py:32
  332.4 6.1 %collective-permute-start.4 = (f32[6,16,18,1]{2,1,3,0:T(8,128)S(1)}, f32[6,16,18,1]{2,1,3,0:T(8,128)}, u32[]{:S(2)}, u32[]{:S(2)}) collective-permute-start(f32[6,16,18,1]{2,1,3,0:T(8,128)S(1)} %copy.7), channel_id=1, source_target_pairs={{1,0},{3,2},{5,4},{7,6},{9,8},{11,10},{13,12},{15,14},{17,16},{19,... | collective-permute-start | bytes 20744 | tf_op jit(solution)/shard_map/ppermute | solution.py:33
  339.9 2.3 copy-start.3
  339.9 2.3 copy-start.5
  342.3 1.0 copy-start.1
  342.3 1.0 copy-start.11
  342.3 1.0 copy-start.13
  345.3 6.5 %collective-permute-start.6 = (f32[6,16,1,128]{3,2,1,0:T(1,128)S(1)}, f32[6,16,1,128]{3,2,1,0:T(1,128)S(1)}, u32[]{:S(2)}, u32[]{:S(2)}) collective-permute-start(f32[6,16,1,128]{3,2,1,0:T(1,128)S(1)} %get-tuple-element.6), channel_id=1, source_target_pairs={{0,2},{2,4},{4,6},{6,8},{8,10},{10,12},{12,14},{14,16},{16,18},{18... | collective-permute-start | bytes 147464 | tf_op jit(solution)/shard_map/ppermute | solution.py:32
  347.2 6.3 %collective-permute-start.7 = (f32[6,16,1,128]{3,2,1,0:T(1,128)S(1)}, f32[6,16,1,128]{3,2,1,0:T(1,128)S(1)}, u32[]{:S(2)}, u32[]{:S(2)}) collective-permute-start(f32[6,16,1,128]{3,2,1,0:T(1,128)S(1)} %get-tuple-element.7), channel_id=1, source_target_pairs={{2,0},{4,2},{6,4},{8,6},{10,8},{12,10},{14,12},{16,14},{18,16},{20... | collective-permute-start | bytes 147464 | tf_op jit(solution)/shard_map/ppermute | solution.py:33
  357.0 5.4 %collective-permute-start.8 = (f32[6,16,18,1]{2,1,3,0:T(8,128)S(1)}, f32[6,16,18,1]{2,1,3,0:T(8,128)S(1)}, u32[]{:S(2)}, u32[]{:S(2)}) collective-permute-start(f32[6,16,18,1]{2,1,3,0:T(8,128)S(1)} %copy.12), channel_id=1, source_target_pairs={{0,1},{2,3},{4,5},{6,7},{8,9},{10,11},{12,13},{14,15},{16,17},{18,... | collective-permute-start | bytes 20744 | tf_op jit(solution)/shard_map/ppermute | solution.py:32
  361.0 6.2 %collective-permute-start.9 = (f32[6,16,18,1]{2,1,3,0:T(8,128)S(1)}, f32[6,16,18,1]{2,1,3,0:T(8,128)S(1)}, u32[]{:S(2)}, u32[]{:S(2)}) collective-permute-start(f32[6,16,18,1]{2,1,3,0:T(8,128)S(1)} %copy.13), channel_id=1, source_target_pairs={{1,0},{3,2},{5,4},{7,6},{9,8},{11,10},{13,12},{15,14},{17,16},{19,... | collective-permute-start | bytes 20744 | tf_op jit(solution)/shard_map/ppermute | solution.py:33
  368.9 2.7 copy-start.4
  368.9 2.8 copy-start.6
  371.7 1.3 copy-start
  371.7 1.3 copy-start.2
Sparse Core Ops, SparseCore 0:
  16.8 274.8 all-gather.1
